TPU v7x, 32 devices: a whole 2x2x4 slice. The times are simulated.
32 devices in a mesh: gx: 16 (over z, y, x), gy: 2 (over core).
Axes of the slice: x: 2, y: 2, z: 4, core: 2. Of those that a mesh axis runs over, the one named last changes fastest.
Arguments:
- features: bfloat16 [16, 2, 2, 512, 128], P('gx', 'gy'), may hold values from -6 to 6
- cotangent: bfloat16 [16, 2, 2, 512, 128], P('gx', 'gy'), may hold values from -6 to 6
- neighbours: int32 [16, 2, 2, 27], P('gx', 'gy'), may hold values from -1 to 17, as said below
- weights: bfloat16 [27, 128, 128], replicated, may hold values from -0.109375 to 0.109375
- channel_gain: float32 [128], replicated, may hold values from 0.5 to 2
Outputs:
- output: bfloat16 [16, 2, 2, 512, 128], P('gx', 'gy')
- input_grad: bfloat16 [16, 2, 2, 512, 128], P('gx', 'gy')
- weight_grad: float32 [27, 128, 128], replicated
- gain_grad: float32 [128], replicated
Inputs may be any that keep to these rules, and one draw needn't show every extreme that they name: `neighbours`: entry [i, j, s, k] names, for slot s of device (i, j) and direction k = 9 (a + 1) + 3 (b + 1) + (c + 1), the block at block offset (a, b, c): the code (3 (i2 - i + 1) + (j2 - j + 1)) * 2 + s2 for slot s2 of device (i2, j2), always equal or beside (i, j), with i2 - i equal to 0 or a and j2 - j equal to 0 or b, or -1 where no occupied block lies. Codes are therefore at most 17. Entry 13 is 8 + s for an occupied slot; an empty slot has -1 everywhere. The relation is symmetric: the block named in direction k names the first one back in direction 26 - k. Some device has all 2 slots occupied.
All inputs are finite; a program needn't handle non-finite values.
Results may differ from a plain program's by a relative error of at most 0.0042.
Values may be sent and summed in bfloat16 or wider, within the bound.
A program may use at most 64 MiB of HBM per device.

v0:
```python
from functools import partial
import jax
import jax.numpy as jnp
from jax import lax
from jax.sharding import PartitionSpec as P

DIRECTIONS = [(a, b, c) for a in (-1, 0, 1) for b in (-1, 0, 1) for c in (-1, 0, 1)]


def padded(value, sides, width):
    for axis, dim in sides:
        count, length = (lax.axis_size(axis), value.shape[dim])
        up = [(i, (i + 1) % count) for i in range(count - 1)]
        down = [(j, i) for i, j in up]
        last = lax.slice_in_dim(value, length - width, length, axis=dim)
        leading = lax.slice_in_dim(value, 0, width, axis=dim)
        before = lax.ppermute(last, axis, up)
        after = lax.ppermute(leading, axis, down)
        value = jnp.concatenate([before, value, after], axis=dim)
    return value


def rim_bounds(d):
    if d < 0:
        return (7, 8)
    if d == 0:
        return (0, 8)
    return (0, 1)


def rim_range(d):
    lower, upper = rim_bounds(d)
    return slice(lower, upper)


def region_of(gathered_table, use_faces, a, b, c):
    return gathered_table[:, rim_range(a), rim_range(b), rim_range(c)]


def assemble(own_blocks, region_fn, slot_codes):
    planes = []
    for a in (-1, 0, 1):
        row_parts = []
        for b in (-1, 0, 1):
            col_parts = []
            for c in (-1, 0, 1):
                k = (a + 1) * 9 + (b + 1) * 3 + (c + 1)
                if k == 13:
                    block_piece = own_blocks
                else:
                    region = region_fn(a, b, c)
                    block_piece = jnp.take(region, jnp.maximum(slot_codes[:, k], 0), axis=0)
                    present = (slot_codes[:, k] >= 0)[:, None, None, None, None]
                    block_piece = jnp.where(present, block_piece, jnp.zeros((), block_piece.dtype))
                col_parts.append(block_piece)
            row_parts.append(jnp.concatenate(col_parts, axis=3))
        planes.append(jnp.concatenate(row_parts, axis=2))
    return jnp.concatenate(planes, axis=1)


def window(padded_tile, a, b, c):
    capacity = padded_tile.shape[0]
    channels = padded_tile.shape[-1]
    return padded_tile[:, 1 + a : 9 + a, 1 + b : 9 + b, 1 + c : 9 + c].reshape(
        capacity * 512, channels
    )


def convolve(padded_tile, weights):
    total = None
    for k in range(27):
        a, b, c = DIRECTIONS[k]
        term = jnp.dot(window(padded_tile, a, b, c), weights[k], preferred_element_type=jnp.float32)
        total = term if total is None else total + term
    return total


def convolve_adjoint(padded_tile, weights):
    total = None
    for k in range(27):
        a, b, c = DIRECTIONS[k]
        term = lax.dot_general(
            window(padded_tile, -a, -b, -c),
            weights[k],
            (((1,), (1,)), ((), ())),
            preferred_element_type=jnp.float32,
        )
        total = term if total is None else total + term
    return total


def weight_terms(padded_tile, scaled):
    terms = []
    for k in range(27):
        a, b, c = DIRECTIONS[k]
        terms.append(
            lax.dot_general(
                window(padded_tile, a, b, c),
                scaled,
                (((0,), (0,)), ((), ())),
                preferred_element_type=jnp.float32,
            )
        )
    return jnp.stack(terms, axis=0)


def forward_table(own_blocks):
    capacity = own_blocks.shape[0]
    channels = own_blocks.shape[-1]
    sent = own_blocks.reshape(1, 1, capacity, 512, channels)
    received = padded(sent, (("gx", 0), ("gy", 1)), 1)
    return partial(region_of, received.reshape(9 * capacity, 8, 8, 8, channels), False)


def backward_table(own_blocks):
    capacity = own_blocks.shape[0]
    channels = own_blocks.shape[-1]
    sent = own_blocks.reshape(1, 1, capacity, 512, channels)
    received = padded(sent, (("gx", 0), ("gy", 1)), 1)
    return partial(region_of, received.reshape(9 * capacity, 8, 8, 8, channels), False)


def on_device(features, cotangent, neighbours, weights, channel_gain):
    slot_codes = neighbours[0, 0]
    capacity = features.shape[2]
    channels = features.shape[-1]
    occupied = (slot_codes[:, 13] >= 0)[:, None, None]
    own_x = jnp.where(occupied, features[0, 0], jnp.zeros((), features.dtype)).reshape(
        capacity, 8, 8, 8, channels
    )
    regions_x = forward_table(own_x)
    tile_x = assemble(own_x, regions_x, slot_codes)
    conv_out = convolve(tile_x, weights)
    pre_act = own_x.reshape(-1, channels).astype(jnp.float32) + channel_gain * conv_out
    sigmoid_value = jax.nn.sigmoid(pre_act)
    result = (pre_act * sigmoid_value).astype(jnp.bfloat16)
    upstream = (
        jnp.where(occupied, cotangent[0, 0], jnp.zeros((), cotangent.dtype))
        .reshape(-1, channels)
        .astype(jnp.float32)
    )
    pre_grad = upstream * sigmoid_value * (1.0 + pre_act * (1.0 - sigmoid_value))
    scaled = (channel_gain * pre_grad).astype(jnp.bfloat16)
    own_u = scaled.reshape(capacity, 8, 8, 8, channels)
    regions_u = backward_table(own_u)
    tile_u = assemble(own_u, regions_u, slot_codes)
    grad_here = (pre_grad + convolve_adjoint(tile_u, weights)).astype(jnp.bfloat16)
    local_weight = weight_terms(tile_x, scaled)
    local_gain = jnp.sum(pre_grad * conv_out, axis=0)
    weight_grad, gain_grad = lax.psum((local_weight, local_gain), ("gx", "gy"))
    return (
        result.reshape(1, 1, capacity, 512, channels),
        grad_here.reshape(1, 1, capacity, 512, channels),
        weight_grad,
        gain_grad,
    )


def solution(mesh):
    in_specs = (
        P("gx", "gy", None, None, None),
        P("gx", "gy", None, None, None),
        P("gx", "gy", None, None),
        P(),
        P(),
    )
    out_specs = (P("gx", "gy", None, None, None), P("gx", "gy", None, None, None), P(), P())
    return jax.shard_map(
        on_device, mesh=mesh, in_specs=in_specs, out_specs=out_specs, check_vma=False
    )
```

profile of v0, /device:TPU:0, one launch (start us, length us, event | category | flops | bytes accessed | tf_op | source)
XLA Modules:
  0.0 304.9 jit_solution(12972801754330378274)
XLA Ops:
  7.2 1.8 compare_reduce_fusion.25
  10.1 4.9 %collective-permute-start = (bf16[1,1,2,512,128]{4,3,2,1,0:T(8,128)(2,1)S(1)}, bf16[1,1,2,512,128]{4,3,2,1,0:T(8,128)(2,1)S(1)}, u32[]{:S(2)}, u32[]{:S(2)}) collective-permute-start(bf16[1,1,2,512,128]{4,3,2,1,0:T(8,128)(2,1)S(1)} %broadcast_select_fusion.1), channel_id=1, source_target_pairs={{0,2},{2,4},{4,6},{6,8},{8,10},{10,12},{12,14},{14,16},{16,18},{18... | collective-permute-start | bytes 786440 | tf_op jit(solution)/shard_map/ppermute | solution.py:17
  16.3 1.9 maximum_reduce_fusion.8
  18.2 2.5 compare_reduce_fusion.8
  48.6 1.5 collective-permute-start.2
  50.1 1.5 collective-permute-start.3
  79.8 1.5 copy.266
  81.3 1.4 gather_fusion.3
  97.2 1.4 gather_fusion.7
  98.6 1.4 gather_fusion.1
  100.1 1.6 gather_fusion.4
  101.7 1.5 gather_fusion.18
  122.6 4.4 %collective-permute-start.4 = (bf16[1,1,2,512,128]{4,3,2,1,0:T(8,128)(2,1)S(1)}, bf16[1,1,2,512,128]{4,3,2,1,0:T(8,128)(2,1)S(1)}, u32[]{:S(2)}, u32[]{:S(2)}) collective-permute-start(bf16[1,1,2,512,128]{4,3,2,1,0:T(8,128)(2,1)S(1)} %bitcast.836), channel_id=1, source_target_pairs={{0,2},{2,4},{4,6},{6,8},{8,10},{10,12},{12,14},{14,16},{16,18},{18... | collective-permute-start | bytes 786440 | tf_op jit(solution)/shard_map/ppermute | solution.py:17
  127.0 1.5 collective-permute-start.5
  149.3 2.0 collective-permute-start.6
  156.2 44.2 %psum.15 = f32[128]{0:T(128)} all-reduce(f32[128]{0:T(128)S(1)} %get-tuple-element.64), channel_id=1, replica_groups=mesh['gx'=16,'gy'=2] {'gx','gy'}, use_global_device_ids=true, to_apply=%region_2.10 | all-reduce | flops 128 | bytes 1024 | tf_op jit(solution)/shard_map/psum | solution.py:150
  212.8 1.6 gather_fusion.27
  224.0 1.5 gather_fusion.35
  229.2 1.4 gather_fusion.50
  230.7 1.4 gather_fusion.41
  232.1 1.6 gather_fusion.38
  238.1 1.4 gather_fusion.44
  255.6 39.6 %all-reduce.2.cloned.1.call-done = f32[27,128,128]{2,1,0:T(8,128)} async-done(((f32[27,128,128]{2,1,0:T(8,128)}), f32[27,128,128]{2,1,0:T(8,128)}) %all-reduce.2.cloned.1.call-update) | async-done | bytes 1769488 | tf_op jit(solution)/shard_map/psum | solution.py:150
  295.1 2.9 copy.308
  (484 shorter events, 162.6 us)
Async XLA Ops:
  7.2 46.1 %copy-start.1 = (bf16[1,1,2,512,128]{4,3,2,1,0:T(8,128)(2,1)S(1)}, bf16[1,1,2,512,128]{4,3,2,1,0:T(8,128)(2,1)}, u32[]{:S(2)}) copy-start(bf16[1,1,2,512,128]{4,3,2,1,0:T(8,128)(2,1)} %param.19) | copy-start | bytes 786436
  7.2 288.0 %all-reduce.2.cloned.1.call-start = ((), (), s32[]{:S(2)}) async-start(), calls=%async_computation | async-start | bytes 3538944 | tf_op jit(solution)/shard_map/psum | solution.py:150
  10.1 38.4 %collective-permute-start = (bf16[1,1,2,512,128]{4,3,2,1,0:T(8,128)(2,1)S(1)}, bf16[1,1,2,512,128]{4,3,2,1,0:T(8,128)(2,1)S(1)}, u32[]{:S(2)}, u32[]{:S(2)}) collective-permute-start(bf16[1,1,2,512,128]{4,3,2,1,0:T(8,128)(2,1)S(1)} %broadcast_select_fusion.1), channel_id=1, source_target_pairs={{0,2},{2,4},{4,6},{6,8},{8,10},{10,12},{12,14},{14,16},{16,18},{18... | collective-permute-start | bytes 786440 | tf_op jit(solution)/shard_map/ppermute | solution.py:17
  15.0 33.5 %collective-permute-start.1 = (bf16[1,1,2,512,128]{4,3,2,1,0:T(8,128)(2,1)S(1)}, bf16[1,1,2,512,128]{4,3,2,1,0:T(8,128)(2,1)S(1)}, u32[]{:S(2)}, u32[]{:S(2)}) collective-permute-start(bf16[1,1,2,512,128]{4,3,2,1,0:T(8,128)(2,1)S(1)} %broadcast_select_fusion.1), channel_id=1, source_target_pairs={{2,0},{4,2},{6,4},{8,6},{10,8},{12,10},{14,12},{16,14},{18,16},{20... | collective-permute-start | bytes 786440 | tf_op jit(solution)/shard_map/ppermute | solution.py:18
  18.2 41.5 %copy-start.45 = (pred[2]{0:T(512)(128)(4,1)}, pred[2]{0:T(512)(128)(4,1)S(1)}, u32[]{:S(2)}) copy-start(pred[2]{0:T(512)(128)(4,1)S(1)} %compare_and_fusion.16) | copy-start | bytes 10
  20.7 39.1 %copy-start.33 = (pred[2]{0:T(512)(128)(4,1)}, pred[2]{0:T(512)(128)(4,1)S(1)}, u32[]{:S(2)}) copy-start(pred[2]{0:T(512)(128)(4,1)S(1)} %get-tuple-element.46) | copy-start | bytes 10
  20.7 39.8 %copy-start.31 = (pred[2]{0:T(512)(128)(4,1)}, pred[2]{0:T(512)(128)(4,1)S(1)}, u32[]{:S(2)}) copy-start(pred[2]{0:T(512)(128)(4,1)S(1)} %get-tuple-element.44) | copy-start | bytes 10
  34.7 24.5 %copy-start.20 = (s32[1024]{0:T(1024)}, s32[1024]{0:T(1024)S(1)}, u32[]{:S(2)}) copy-start(s32[1024]{0:T(1024)S(1)} %pad_clamp_fusion.16) | copy-start | bytes 12292
  34.7 25.1 %copy-start.19 = (s32[1024]{0:T(1024)}, s32[1024]{0:T(1024)S(1)}, u32[]{:S(2)}) copy-start(s32[1024]{0:T(1024)S(1)} %pad_clamp_fusion.14) | copy-start | bytes 12292
  35.3 25.2 %copy-start.18 = (s32[1024]{0:T(1024)}, s32[1024]{0:T(1024)S(1)}, u32[]{:S(2)}) copy-start(s32[1024]{0:T(1024)S(1)} %pad_clamp_fusion.11) | copy-start | bytes 12292
  48.6 4.8 %collective-permute-start.2 = (bf16[3,1,2,512,128]{4,3,2,1,0:T(8,128)(2,1)S(1)}, bf16[3,1,2,512,128]{4,3,2,1,0:T(8,128)(2,1)S(1)}, u32[]{:S(2)}, u32[]{:S(2)}) collective-permute-start(bf16[3,1,2,512,128]{4,3,2,1,0:T(8,128)(2,1)S(1)} %pad_maximum_fusion.2), channel_id=1, source_target_pairs={{0,1},{2,3},{4,5},{6,7},{8,9},{10,11},{12,13},{14,15},{16,17},{18,... | collective-permute-start | bytes 2359304 | tf_op jit(solution)/shard_map/ppermute | solution.py:17
  50.1 4.2 %collective-permute-start.3 = (bf16[3,1,2,512,128]{4,3,2,1,0:T(8,128)(2,1)S(1)}, bf16[3,1,2,512,128]{4,3,2,1,0:T(8,128)(2,1)S(1)}, u32[]{:S(2)}, u32[]{:S(2)}) collective-permute-start(bf16[3,1,2,512,128]{4,3,2,1,0:T(8,128)(2,1)S(1)} %pad_maximum_fusion.2), channel_id=1, source_target_pairs={{1,0},{3,2},{5,4},{7,6},{9,8},{11,10},{13,12},{15,14},{17,16},{19,... | collective-permute-start | bytes 2359304 | tf_op jit(solution)/shard_map/ppermute | solution.py:18
  68.3 14.4 %copy-start.38 = (pred[2]{0:T(512)(128)(4,1)S(1)}, pred[2]{0:T(512)(128)(4,1)}, u32[]{:S(2)}) copy-start(pred[2]{0:T(512)(128)(4,1)} %get-tuple-element.60) | copy-start | bytes 10
  68.4 20.6 %copy-start.12 = (bf16[18,1,1,1,128]{4,3,2,1,0:T(2,128)(2,1)S(1)}, bf16[18,1,1,1,128]{4,3,2,1,0:T(2,128)(2,1)}, u32[]{:S(2)}) copy-start(bf16[18,1,1,1,128]{4,3,2,1,0:T(2,128)(2,1)} %get-tuple-element.100) | copy-start | bytes 13828
  68.4 22.6 %copy-start.11 = (bf16[18,1,1,1,128]{4,3,2,1,0:T(2,128)(2,1)S(1)}, bf16[18,1,1,1,128]{4,3,2,1,0:T(2,128)(2,1)}, u32[]{:S(2)}) copy-start(bf16[18,1,1,1,128]{4,3,2,1,0:T(2,128)(2,1)} %get-tuple-element.98) | copy-start | bytes 13828
  122.6 25.7 %collective-permute-start.4 = (bf16[1,1,2,512,128]{4,3,2,1,0:T(8,128)(2,1)S(1)}, bf16[1,1,2,512,128]{4,3,2,1,0:T(8,128)(2,1)S(1)}, u32[]{:S(2)}, u32[]{:S(2)}) collective-permute-start(bf16[1,1,2,512,128]{4,3,2,1,0:T(8,128)(2,1)S(1)} %bitcast.836), channel_id=1, source_target_pairs={{0,2},{2,4},{4,6},{6,8},{8,10},{10,12},{12,14},{14,16},{16,18},{18... | collective-permute-start | bytes 786440 | tf_op jit(solution)/shard_map/ppermute | solution.py:17
  127.0 21.4 %collective-permute-start.5 = (bf16[1,1,2,512,128]{4,3,2,1,0:T(8,128)(2,1)S(1)}, bf16[1,1,2,512,128]{4,3,2,1,0:T(8,128)(2,1)S(1)}, u32[]{:S(2)}, u32[]{:S(2)}) collective-permute-start(bf16[1,1,2,512,128]{4,3,2,1,0:T(8,128)(2,1)S(1)} %bitcast.837), channel_id=1, source_target_pairs={{2,0},{4,2},{6,4},{8,6},{10,8},{12,10},{14,12},{16,14},{18,16},{20... | collective-permute-start | bytes 786440 | tf_op jit(solution)/shard_map/ppermute | solution.py:18
  149.3 51.1 %collective-permute-start.6 = (bf16[3,1,2,512,128]{4,3,2,1,0:T(8,128)(2,1)}, bf16[3,1,2,512,128]{4,3,2,1,0:T(8,128)(2,1)S(1)}, u32[]{:S(2)}, u32[]{:S(2)}) collective-permute-start(bf16[3,1,2,512,128]{4,3,2,1,0:T(8,128)(2,1)} %pad_maximum_fusion.3), channel_id=1, source_target_pairs={{0,1},{2,3},{4,5},{6,7},{8,9},{10,11},{12,13},{14,15},{16,17},{18,... | collective-permute-start | bytes 2359304 | tf_op jit(solution)/shard_map/ppermute | solution.py:17
  151.3 49.1 %collective-permute-start.7 = (bf16[3,1,2,512,128]{4,3,2,1,0:T(8,128)(2,1)}, bf16[3,1,2,512,128]{4,3,2,1,0:T(8,128)(2,1)}, u32[]{:S(2)}, u32[]{:S(2)}) collective-permute-start(bf16[3,1,2,512,128]{4,3,2,1,0:T(8,128)(2,1)} %pad_maximum_fusion.3), channel_id=1, source_target_pairs={{1,0},{3,2},{5,4},{7,6},{9,8},{11,10},{13,12},{15,14},{17,16},{19,... | collective-permute-start | bytes 2359304 | tf_op jit(solution)/shard_map/ppermute | solution.py:18
  220.1 13.7 %copy-start.21 = (pred[2]{0:T(512)(128)(4,1)S(1)}, pred[2]{0:T(512)(128)(4,1)}, u32[]{:S(2)}) copy-start(pred[2]{0:T(512)(128)(4,1)} %get-tuple-element.35) | copy-start | bytes 10
  220.1 16.5 %copy-start.16 = (bf16[18,1,1,1,128]{4,3,2,1,0:T(2,128)(2,1)S(1)}, bf16[18,1,1,1,128]{4,3,2,1,0:T(2,128)(2,1)}, u32[]{:S(2)}) copy-start(bf16[18,1,1,1,128]{4,3,2,1,0:T(2,128)(2,1)} %get-tuple-element.67) | copy-start | bytes 13828
  220.1 16.5 %copy-start.17 = (bf16[18,1,1,1,128]{4,3,2,1,0:T(2,128)(2,1)S(1)}, bf16[18,1,1,1,128]{4,3,2,1,0:T(2,128)(2,1)}, u32[]{:S(2)}) copy-start(bf16[18,1,1,1,128]{4,3,2,1,0:T(2,128)(2,1)} %get-tuple-element.72) | copy-start | bytes 13828
  220.2 20.1 %copy-start.6 = (bf16[18,1,8,1,128]{4,3,2,1,0:T(2,128)(2,1)S(1)}, bf16[18,1,8,1,128]{4,3,2,1,0:T(2,128)(2,1)}, u32[]{:S(2)}) copy-start(bf16[18,1,8,1,128]{4,3,2,1,0:T(2,128)(2,1)} %get-tuple-element.82) | copy-start | bytes 110596
  220.2 24.4 %copy-start.25 = (pred[2]{0:T(512)(128)(4,1)S(1)}, pred[2]{0:T(512)(128)(4,1)}, u32[]{:S(2)}) copy-start(pred[2]{0:T(512)(128)(4,1)} %get-tuple-element.59) | copy-start | bytes 10
  (38 other events, 157.3 us)
Sparse Core Ops, SparseCore 0:
  156.3 138.7 all-reduce.1
where the time goes:
time: 307 us; the launch traced here: 305 us
  local copies, waits for them, and re-layouts  76.8 us (25%)
  other arithmetic  72.2 us (24%)
  blocking collectives  44.2 us (14%)
  waiting for transfers between devices  40.5 us (13%)
  matrix products  37.2 us (12%)
  starting transfers between devices  18.4 us (6%)
  between operations  15.7 us (5%)
    gather x52, local copies, waits for them, and re-layouts, assemble(): block_piece = jnp.take(region, jnp.maximum(slot_codes[:, k], 0), axis=0)  45.4 us
    psum x1, blocking collectives, on_device(): weight_grad, gain_grad = lax.psum((local_weight, local_gain), ('gx', 'gy'))  44.2 us
    psum x1, waiting for transfers between devices, on_device(): weight_grad, gain_grad = lax.psum((local_weight, local_gain), ('gx', 'gy'))  39.6 us
    select_n x42, other arithmetic, assemble(): jnp.where(present, block_piece, jnp.zeros((), block_piece.dtype))  25.5 us
    dot_general x27, matrix products, weight_terms(): lax.dot_general(window(padded_tile, a, b, c), scaled, (((0,), (0,)), ((),...  24.3 us
    and x26, other arithmetic, assemble(): block_piece = jnp.take(region, jnp.maximum(slot_codes[:, k], 0), axis=0)  13.8 us
    gather x26, other arithmetic  13.7 us
    ppermute x4, starting transfers between devices, padded(): before = lax.ppermute(last, axis, up)  12.8 us
  transfers between devices with their start and end apart: 9, of which 2 were waited for; matrix products, arithmetic and copies ran while one was open for 36% of the time, Pallas kernels for 0%

commit v1 on v0

--- a/solution.py
+++ b/solution.py
@@ -147,7 +147,7 @@
     grad_here = (pre_grad + convolve_adjoint(tile_u, weights)).astype(jnp.bfloat16)
     local_weight = weight_terms(tile_x, scaled)
     local_gain = jnp.sum(pre_grad * conv_out, axis=0)
-    weight_grad, gain_grad = lax.psum((local_weight, local_gain), ("gx", "gy"))
+    weight_grad, gain_grad = lax.psum(lax.psum((local_weight, local_gain), "gy"), "gx")
     return (
         result.reshape(1, 1, capacity, 512, channels),
         grad_here.reshape(1, 1, capacity, 512, channels),

time: 307 us -> 404 us (1.32)
  waiting for transfers between devices: 40.5 us -> 115 us
  local copies, waits for them, and re-layouts: 76.8 us -> 90.3 us
    psum x1 -> x2, waiting for transfers between devices: 39.6 us -> 114 us  [the longest x1 114 us: on_device(): lax.psum(lax.psum((local_weight, local_gain), 'gy'), 'gx')]
    select_n x36, local copies, waits for them, and re-layouts: 4.35 us -> 10.8 us  [assemble(): jnp.where(present, block_piece, jnp.zeros((), block_piece.dtype))]
    select_n x42, other arithmetic: 25.5 us -> 29.9 us  [assemble(): jnp.where(present, block_piece, jnp.zeros((), block_piece.dtype))]
    psum x1 -> x2, blocking collectives: 44.2 us -> 47.5 us  [the longest x1 43.4 us: on_device(): lax.psum(lax.psum((local_weight, local_gain), 'gy'), 'gx')]
    unnamed x141 -> x109, local copies, waits for them, and re-layouts: 12.4 us -> 15.5 us
  transfers between devices with their start and end apart: 9 -> 10, of which waited for: 2 -> 2; matrix products, arithmetic and copies ran while one was open for 36% -> 32% of each run, Pallas kernels for 0% -> 0%
where the time goes in v1:
time: 404 us; the launch traced here: 401 us
  waiting for transfers between devices  115 us (28%)
  local copies, waits for them, and re-layouts  90.3 us (22%)
  other arithmetic  76.2 us (19%)
  blocking collectives  47.5 us (12%)
  matrix products  37.2 us (9%)
  starting transfers between devices  18.4 us (5%)
  between operations  15.6 us (4%)
    psum x1, waiting for transfers between devices, on_device(): lax.psum(lax.psum((local_weight, local_gain), 'gy'), 'gx')  114 us
    gather x52, local copies, waits for them, and re-layouts, assemble(): block_piece = jnp.take(region, jnp.maximum(slot_codes[:, k], 0), axis=0)  48.7 us
    psum x1, blocking collectives, on_device(): lax.psum(lax.psum((local_weight, local_gain), 'gy'), 'gx')  43.4 us
    select_n x42, other arithmetic, assemble(): jnp.where(present, block_piece, jnp.zeros((), block_piece.dtype))  29.9 us
    dot_general x27, matrix products, weight_terms(): lax.dot_general(window(padded_tile, a, b, c), scaled, (((0,), (0,)), ((),...  24.3 us
    unnamed x109, local copies, waits for them, and re-layouts  15.5 us
    ppermute x4, starting transfers between devices, padded(): before = lax.ppermute(last, axis, up)  12.8 us
    and x26, other arithmetic, assemble(): block_piece = jnp.take(region, jnp.maximum(slot_codes[:, k], 0), axis=0)  12.1 us
  transfers between devices with their start and end apart: 10, of which 2 were waited for; matrix products, arithmetic and copies ran while one was open for 32% of the time, Pallas kernels for 0%

profile of v1, /device:TPU:0, one launch (start us, length us, event | category | flops | bytes accessed | tf_op | source)
XLA Modules:
  0.0 400.7 jit_solution(16233124864499728577)
XLA Ops:
  7.2 1.8 compare_reduce_fusion.25
  10.1 4.9 %collective-permute-start = (bf16[1,1,2,512,128]{4,3,2,1,0:T(8,128)(2,1)S(1)}, bf16[1,1,2,512,128]{4,3,2,1,0:T(8,128)(2,1)S(1)}, u32[]{:S(2)}, u32[]{:S(2)}) collective-permute-start(bf16[1,1,2,512,128]{4,3,2,1,0:T(8,128)(2,1)S(1)} %broadcast_select_fusion.1), channel_id=1, source_target_pairs={{0,2},{2,4},{4,6},{6,8},{8,10},{10,12},{12,14},{14,16},{16,18},{18... | collective-permute-start | bytes 786440 | tf_op jit(solution)/shard_map/ppermute | solution.py:17
  16.3 1.9 maximum_reduce_fusion.8
  18.2 2.5 compare_reduce_fusion.8
  44.1 1.5 collective-permute-start.2
  45.6 1.5 collective-permute-start.3
  60.2 1.5 gather_fusion.10
  75.8 1.5 copy.266
  93.2 1.4 gather_fusion.7
  94.6 1.4 gather_fusion.1
  96.1 1.6 gather_fusion.4
  97.7 1.5 gather_fusion.18
  118.5 4.4 %collective-permute-start.4 = (bf16[1,1,2,512,128]{4,3,2,1,0:T(8,128)(2,1)S(1)}, bf16[1,1,2,512,128]{4,3,2,1,0:T(8,128)(2,1)S(1)}, u32[]{:S(2)}, u32[]{:S(2)}) collective-permute-start(bf16[1,1,2,512,128]{4,3,2,1,0:T(8,128)(2,1)S(1)} %bitcast.836), channel_id=1, source_target_pairs={{0,2},{2,4},{4,6},{6,8},{8,10},{10,12},{12,14},{14,16},{16,18},{18... | collective-permute-start | bytes 786440 | tf_op jit(solution)/shard_map/ppermute | solution.py:17
  122.9 1.5 collective-permute-start.5
  145.2 2.0 collective-permute-start.6
  152.2 4.1 %psum.30 = f32[128]{0:T(128)S(1)} all-reduce(f32[128]{0:T(128)S(1)} %get-tuple-element.64), channel_id=1, replica_groups=mesh['gx'=16,'gy'=2] {'gy'}, use_global_device_ids=true, to_apply=%region_3.11 | all-reduce | flops 128 | bytes 1024 | tf_op jit(solution)/shard_map/psum | solution.py:150
  156.4 43.4 %psum.31 = f32[128]{0:T(128)} all-reduce(f32[128]{0:T(128)S(1)} %psum.30), channel_id=1, replica_groups=mesh['gx'=16,'gy'=2] {'gx'}, use_global_device_ids=true, to_apply=%region_4.12 | all-reduce | flops 128 | bytes 1024 | tf_op jit(solution)/shard_map/psum | solution.py:150
  233.6 2.0 gather_fusion.50
  235.7 2.0 gather_fusion.41
  237.7 1.6 gather_fusion.38
  258.5 1.6 gather_fusion.47
  265.2 1.5 maximum_maximum_fusion.1
  276.5 114.4 %all-reduce.5.cloned.1.call-done = f32[27,128,128]{2,1,0:T(8,128)} async-done(((f32[27,128,128]{2,1,0:T(8,128)}), f32[27,128,128]{2,1,0:T(8,128)}) %all-reduce.5.cloned.1.call-update) | async-done | bytes 1769488 | tf_op jit(solution)/shard_map/psum | solution.py:150
  391.0 2.9 copy.309
  (456 shorter events, 180.4 us)
Async XLA Ops:
  7.2 41.6 %copy-start.1 = (bf16[1,1,2,512,128]{4,3,2,1,0:T(8,128)(2,1)S(1)}, bf16[1,1,2,512,128]{4,3,2,1,0:T(8,128)(2,1)}, u32[]{:S(2)}) copy-start(bf16[1,1,2,512,128]{4,3,2,1,0:T(8,128)(2,1)} %param.19) | copy-start | bytes 786436
  7.2 266.5 %all-reduce.3.cloned.1.call-start = ((), (), s32[]{:S(2)}) async-start(), calls=%async_computation | async-start | bytes 3538944 | tf_op jit(solution)/shard_map/psum | solution.py:150
  10.1 33.9 %collective-permute-start = (bf16[1,1,2,512,128]{4,3,2,1,0:T(8,128)(2,1)S(1)}, bf16[1,1,2,512,128]{4,3,2,1,0:T(8,128)(2,1)S(1)}, u32[]{:S(2)}, u32[]{:S(2)}) collective-permute-start(bf16[1,1,2,512,128]{4,3,2,1,0:T(8,128)(2,1)S(1)} %broadcast_select_fusion.1), channel_id=1, source_target_pairs={{0,2},{2,4},{4,6},{6,8},{8,10},{10,12},{12,14},{14,16},{16,18},{18... | collective-permute-start | bytes 786440 | tf_op jit(solution)/shard_map/ppermute | solution.py:17
  15.0 29.0 %collective-permute-start.1 = (bf16[1,1,2,512,128]{4,3,2,1,0:T(8,128)(2,1)S(1)}, bf16[1,1,2,512,128]{4,3,2,1,0:T(8,128)(2,1)S(1)}, u32[]{:S(2)}, u32[]{:S(2)}) collective-permute-start(bf16[1,1,2,512,128]{4,3,2,1,0:T(8,128)(2,1)S(1)} %broadcast_select_fusion.1), channel_id=1, source_target_pairs={{2,0},{4,2},{6,4},{8,6},{10,8},{12,10},{14,12},{16,14},{18,16},{20... | collective-permute-start | bytes 786440 | tf_op jit(solution)/shard_map/ppermute | solution.py:18
  18.2 37.7 %copy-start.32 = (pred[2]{0:T(512)(128)(4,1)}, pred[2]{0:T(512)(128)(4,1)S(1)}, u32[]{:S(2)}) copy-start(pred[2]{0:T(512)(128)(4,1)S(1)} %compare_and_fusion.16) | copy-start | bytes 10
  20.7 35.2 %copy-start.26 = (pred[2]{0:T(512)(128)(4,1)}, pred[2]{0:T(512)(128)(4,1)S(1)}, u32[]{:S(2)}) copy-start(pred[2]{0:T(512)(128)(4,1)S(1)} %get-tuple-element.46) | copy-start | bytes 10
  20.7 35.9 %copy-start.25 = (pred[2]{0:T(512)(128)(4,1)}, pred[2]{0:T(512)(128)(4,1)S(1)}, u32[]{:S(2)}) copy-start(pred[2]{0:T(512)(128)(4,1)S(1)} %get-tuple-element.44) | copy-start | bytes 10
  20.7 36.6 %copy-start.24 = (pred[2]{0:T(512)(128)(4,1)}, pred[2]{0:T(512)(128)(4,1)S(1)}, u32[]{:S(2)}) copy-start(pred[2]{0:T(512)(128)(4,1)S(1)} %get-tuple-element.41) | copy-start | bytes 10
  20.7 37.3 %copy-start.23 = (pred[2]{0:T(512)(128)(4,1)}, pred[2]{0:T(512)(128)(4,1)S(1)}, u32[]{:S(2)}) copy-start(pred[2]{0:T(512)(128)(4,1)S(1)} %get-tuple-element.39) | copy-start | bytes 10
  20.7 35.9 %copy-start.33 = (pred[2]{0:T(512)(128)(4,1)}, pred[2]{0:T(512)(128)(4,1)S(1)}, u32[]{:S(2)}) copy-start(pred[2]{0:T(512)(128)(4,1)S(1)} %compare_and_fusion.14) | copy-start | bytes 10
  21.2 36.0 %copy-start.30 = (pred[2]{0:T(512)(128)(4,1)}, pred[2]{0:T(512)(128)(4,1)S(1)}, u32[]{:S(2)}) copy-start(pred[2]{0:T(512)(128)(4,1)S(1)} %compare_and_fusion.11) | copy-start | bytes 10
  21.3 36.7 %copy-start.31 = (pred[2]{0:T(512)(128)(4,1)}, pred[2]{0:T(512)(128)(4,1)S(1)}, u32[]{:S(2)}) copy-start(pred[2]{0:T(512)(128)(4,1)S(1)} %compare_and_fusion.9) | copy-start | bytes 10
  33.1 27.1 %copy-start.12 = (s32[1024]{0:T(1024)}, s32[1024]{0:T(1024)S(1)}, u32[]{:S(2)}) copy-start(s32[1024]{0:T(1024)S(1)} %pad_clamp_fusion.15) | copy-start | bytes 12292
  33.1 24.3 %copy-start.16 = (s32[1024]{0:T(1024)}, s32[1024]{0:T(1024)S(1)}, u32[]{:S(2)}) copy-start(s32[1024]{0:T(1024)S(1)} %pad_clamp_fusion.9) | copy-start | bytes 12292
  33.1 28.6 %copy-start.13 = (s32[1024]{0:T(1024)}, s32[1024]{0:T(1024)S(1)}, u32[]{:S(2)}) copy-start(s32[1024]{0:T(1024)S(1)} %pad_clamp_fusion.10) | copy-start | bytes 12292
  33.2 24.9 %copy-start.15 = (s32[1024]{0:T(1024)}, s32[1024]{0:T(1024)S(1)}, u32[]{:S(2)}) copy-start(s32[1024]{0:T(1024)S(1)} %pad_clamp_fusion.13) | copy-start | bytes 12292
  33.2 25.7 %copy-start.14 = (s32[1024]{0:T(1024)}, s32[1024]{0:T(1024)S(1)}, u32[]{:S(2)}) copy-start(s32[1024]{0:T(1024)S(1)} %pad_clamp_fusion.12) | copy-start | bytes 12292
  44.1 4.8 %collective-permute-start.2 = (bf16[3,1,2,512,128]{4,3,2,1,0:T(8,128)(2,1)S(1)}, bf16[3,1,2,512,128]{4,3,2,1,0:T(8,128)(2,1)S(1)}, u32[]{:S(2)}, u32[]{:S(2)}) collective-permute-start(bf16[3,1,2,512,128]{4,3,2,1,0:T(8,128)(2,1)S(1)} %pad_maximum_fusion.2), channel_id=1, source_target_pairs={{0,1},{2,3},{4,5},{6,7},{8,9},{10,11},{12,13},{14,15},{16,17},{18,... | collective-permute-start | bytes 2359304 | tf_op jit(solution)/shard_map/ppermute | solution.py:17
  45.6 4.2 %collective-permute-start.3 = (bf16[3,1,2,512,128]{4,3,2,1,0:T(8,128)(2,1)S(1)}, bf16[3,1,2,512,128]{4,3,2,1,0:T(8,128)(2,1)S(1)}, u32[]{:S(2)}, u32[]{:S(2)}) collective-permute-start(bf16[3,1,2,512,128]{4,3,2,1,0:T(8,128)(2,1)S(1)} %pad_maximum_fusion.2), channel_id=1, source_target_pairs={{1,0},{3,2},{5,4},{7,6},{9,8},{11,10},{13,12},{15,14},{17,16},{19,... | collective-permute-start | bytes 2359304 | tf_op jit(solution)/shard_map/ppermute | solution.py:18
  118.5 25.7 %collective-permute-start.4 = (bf16[1,1,2,512,128]{4,3,2,1,0:T(8,128)(2,1)S(1)}, bf16[1,1,2,512,128]{4,3,2,1,0:T(8,128)(2,1)S(1)}, u32[]{:S(2)}, u32[]{:S(2)}) collective-permute-start(bf16[1,1,2,512,128]{4,3,2,1,0:T(8,128)(2,1)S(1)} %bitcast.836), channel_id=1, source_target_pairs={{0,2},{2,4},{4,6},{6,8},{8,10},{10,12},{12,14},{14,16},{16,18},{18... | collective-permute-start | bytes 786440 | tf_op jit(solution)/shard_map/ppermute | solution.py:17
  122.9 21.4 %collective-permute-start.5 = (bf16[1,1,2,512,128]{4,3,2,1,0:T(8,128)(2,1)S(1)}, bf16[1,1,2,512,128]{4,3,2,1,0:T(8,128)(2,1)S(1)}, u32[]{:S(2)}, u32[]{:S(2)}) collective-permute-start(bf16[1,1,2,512,128]{4,3,2,1,0:T(8,128)(2,1)S(1)} %bitcast.837), channel_id=1, source_target_pairs={{2,0},{4,2},{6,4},{8,6},{10,8},{12,10},{14,12},{16,14},{18,16},{20... | collective-permute-start | bytes 786440 | tf_op jit(solution)/shard_map/ppermute | solution.py:18
  145.2 54.6 %collective-permute-start.6 = (bf16[3,1,2,512,128]{4,3,2,1,0:T(8,128)(2,1)}, bf16[3,1,2,512,128]{4,3,2,1,0:T(8,128)(2,1)S(1)}, u32[]{:S(2)}, u32[]{:S(2)}) collective-permute-start(bf16[3,1,2,512,128]{4,3,2,1,0:T(8,128)(2,1)} %pad_maximum_fusion.3), channel_id=1, source_target_pairs={{0,1},{2,3},{4,5},{6,7},{8,9},{10,11},{12,13},{14,15},{16,17},{18,... | collective-permute-start | bytes 2359304 | tf_op jit(solution)/shard_map/ppermute | solution.py:17
  147.2 52.5 %collective-permute-start.7 = (bf16[3,1,2,512,128]{4,3,2,1,0:T(8,128)(2,1)}, bf16[3,1,2,512,128]{4,3,2,1,0:T(8,128)(2,1)}, u32[]{:S(2)}, u32[]{:S(2)}) collective-permute-start(bf16[3,1,2,512,128]{4,3,2,1,0:T(8,128)(2,1)} %pad_maximum_fusion.3), channel_id=1, source_target_pairs={{1,0},{3,2},{5,4},{7,6},{9,8},{11,10},{13,12},{15,14},{17,16},{19,... | collective-permute-start | bytes 2359304 | tf_op jit(solution)/shard_map/ppermute | solution.py:18
  152.2 238.8 %all-reduce.5.cloned.1.call-start = ((), (), s32[]{:S(2)}) async-start(), calls=%async_computation.1 | async-start | bytes 3538944 | tf_op jit(solution)/shard_map/psum | solution.py:150
  (23 other events, 159.9 us)
Sparse Core Ops, SparseCore 0:
  152.3 26.1 all-reduce.2
  273.8 117.1 all-reduce.4
